TPU v7x, 32 devices: a whole 2x2x4 slice. The times are simulated.
32 devices in a mesh: group: 2 (over y), scen: 4 (over z), inst: 2 (over x), acct: 2 (over core).
Axes of the slice: x: 2, y: 2, z: 4, core: 2. Of those that a mesh axis runs over, the one named last changes fastest.
Arguments:
- returns: float32 [4096, 1024], P(('group', 'scen')), parts along dimension 0, may hold values from -40 to 40, as said below
- prior: float32 [18, 1024], P('group'), parts along dimension 0, may hold values from -15 to 15
- decay: float32 [1024], replicated, may hold values from 0.000146484375 to 0.06
- seed_var: float32 [1024], replicated, may hold values from 0.2 to 8
- date_offsets: int32 [2048], P('scen'), may hold values from 0 to 2
- block_index: int32 [32768], P(('group', 'inst', 'acct')), parts along dimension 0, may hold values from 0 to 7
- delta_sens: bfloat16 [128, 32768], P(None, ('group', 'inst', 'acct')), parts along dimension 1, may hold values from -0.0625 to 0.0625
- gamma_sens: bfloat16 [128, 32768], P(None, ('group', 'inst', 'acct')), parts along dimension 1, may hold values from -0.0046691895 to 0.0046691895
- positions: bfloat16 [256, 16384], P('group', ('inst', 'acct')), parts along dimension 0, may hold values from -0.09375 to 0.09375
- pattern: int32 [256, 128], P('group', ('inst', 'acct')), parts along dimension 0, may hold values 0 or 1
Outputs:
- acct_pnl: float32 [256, 2048], P(('group', 'scen', 'inst', 'acct')), parts along dimension 0
- margin: float32 [256], P(('group', 'scen', 'inst', 'acct')), parts along dimension 0
There are 2 independent parts, one for each index of `group`. A program takes and returns all parts, laid end to end along the dimension named above; an argument that names none is the same for every part. Nothing has to cross between parts.
Inputs may be any that keep to these rules, and one draw needn't show every extreme that they name: Fat tailed daily returns.
All inputs are finite; a program needn't handle non-finite values. No bound on the sum of `pattern` on one device may be relied on, other than what follows from the above.
Results may differ from a plain program's by a relative error of at most 0.004.
Values sent between devices are 32-bit elements; how exact they have to be, the bound alone decides.
A program may use at most 128 MiB of HBM per device.

v0:
```python
import jax
import jax.numpy as jnp
from jax import lax
from jax.sharding import PartitionSpec as P

WIN = 10


def carried_in(value, axis, join, neutral):
    count, mine = (lax.axis_size(axis), lax.axis_index(axis))
    pieces = jax.tree.map(lambda part: lax.all_gather(part, axis), value)
    subtotal = jax.tree.map(
        lambda part, zero: jnp.full_like(part, 0) + jnp.asarray(zero, part.dtype), value, neutral
    )

    def lap(position, subtotal):
        longer = join(subtotal, jax.tree.map(lambda part: part[position], pieces))
        return jax.tree.map(lambda new, old: jnp.where(position < mine, new, old), longer, subtotal)

    return lax.fori_loop(0, count - 1, lap, subtotal)


def passed_along(value, axis, by):
    peers = lax.axis_size(axis)
    pairs = [(i, i + by) for i in range(peers) if 0 <= i + by < peers]
    return lax.ppermute(value, axis, pairs)


def window_sum(extended, date_offsets, row_count):
    window_total = jnp.zeros((row_count, extended.shape[1]), jnp.float32)
    for lag_step in range(WIN):
        keep_mask = (date_offsets <= lag_step)[:, None]
        window_total = window_total + jnp.where(
            keep_mask, extended[lag_step : lag_step + row_count], 0.0
        )
    return window_total


def combine_chain(earlier, later):
    return (earlier[0] * later[0], later[0] * earlier[1] + later[1])


def body(
    returns,
    prior,
    decay,
    seed_var,
    date_offsets,
    block_index,
    delta_sens,
    gamma_sens,
    positions,
    pattern,
):
    day_rows, factors = returns.shape
    block_len = min(64, day_rows)
    block_count = day_rows // block_len
    highest = lax.Precision.HIGHEST
    log_keep = jnp.log1p(-decay)
    within_step = jnp.arange(1, block_len + 1, dtype=jnp.float32)[:, None]
    growth = jnp.exp(-within_step * log_keep)
    shrink = jnp.exp(within_step * log_keep)
    lower_mask = (jnp.arange(block_len)[:, None] >= jnp.arange(block_len)[None, :]).astype(
        jnp.float32
    )
    drive_terms = (returns * returns * decay).reshape(block_count, block_len, factors)
    cumulated = jnp.einsum("ij,bjf->bif", lower_mask, drive_terms * growth, precision=highest)
    fresh_state = shrink * cumulated
    block_ends = fresh_state[:, -1, :]
    block_gaps = jnp.arange(block_count)[:, None] - jnp.arange(block_count)[None, :] - 1
    gap_power = block_gaps[:, :, None].astype(jnp.float32) * block_len * log_keep
    carry_weight = jnp.where(block_gaps[:, :, None] >= 0, jnp.exp(jnp.minimum(gap_power, 0.0)), 0.0)
    entering = jnp.einsum("bcf,cf->bf", carry_weight, block_ends, precision=highest)
    local_state = (fresh_state + shrink * entering[:, None, :]).reshape(day_rows, factors)
    local_end = local_state[-1]
    span_keep = jnp.exp(day_rows * log_keep)
    prefix_keep, prefix_state = carried_in(
        (span_keep, local_end), "scen", combine_chain, (jnp.ones_like(decay), jnp.zeros_like(decay))
    )
    start_state = prefix_keep * seed_var + prefix_state
    position = jnp.arange(1, day_rows + 1, dtype=jnp.float32)[:, None]
    variance = local_state + jnp.exp(position * log_keep) * start_state
    devices_scen = lax.axis_size("scen")
    scen_rank = lax.axis_index("scen")
    later_days = ((devices_scen - 1 - scen_rank) * day_rows).astype(jnp.float32)
    own_part = jnp.exp(later_days * log_keep) * local_end
    own_part = own_part + jnp.where(
        scen_rank == 0, jnp.exp(devices_scen * day_rows * log_keep) * seed_var, 0.0
    )
    latest = lax.psum(own_part, "scen")
    scaled = returns * jnp.sqrt(latest / variance)
    tail_rows = scaled[day_rows - (WIN - 1) :]
    arrived = passed_along(tail_rows, "scen", 1)
    lead_rows = jnp.where(lax.axis_index("scen") == 0, prior, arrived)
    extended = jnp.concatenate([lead_rows, scaled], axis=0)
    scen_moves = window_sum(extended, date_offsets, day_rows)
    features = jnp.concatenate(
        [scen_moves.astype(jnp.bfloat16), (0.5 * scen_moves * scen_moves).astype(jnp.bfloat16)],
        axis=1,
    )
    inst_count = delta_sens.shape[1]
    block_total = factors // delta_sens.shape[0]
    chosen = block_index[None, :] == jnp.arange(block_total, dtype=jnp.int32)[:, None]
    dense_delta = jnp.where(chosen[:, None, :], delta_sens[None], 0).reshape(factors, inst_count)
    dense_gamma = jnp.where(chosen[:, None, :], gamma_sens[None], 0).reshape(factors, inst_count)
    sensitivity = jnp.concatenate([dense_delta, dense_gamma], axis=0)
    inst_pnl = jnp.dot(features, sensitivity, preferred_element_type=jnp.float32).astype(
        jnp.bfloat16
    )
    acct_total = positions.shape[0]
    held_pos = jnp.where(
        pattern[:, :, None] > 0, positions.reshape(acct_total, pattern.shape[1], -1), 0
    ).reshape(acct_total, inst_count)
    scen_count = lax.axis_size("scen")
    owners = lax.axis_size(("inst", "acct"))
    acct_local = acct_total // (scen_count * owners)
    stacked = held_pos.reshape(scen_count, owners, acct_local, inst_count)
    share_rows = scen_count * acct_local
    acct_term = jnp.einsum("knai,si->nkas", stacked, inst_pnl, preferred_element_type=jnp.float32)
    summed = lax.psum_scatter(
        acct_term.reshape(lax.axis_size(("inst", "acct")) * share_rows, day_rows),
        ("inst", "acct"),
        scatter_dimension=0,
        tiled=True,
    )
    spread = lax.all_to_all(
        summed.reshape(scen_count, acct_local, day_rows),
        "scen",
        split_axis=0,
        concat_axis=2,
        tiled=True,
    )
    acct_pnl = spread.reshape(acct_local, scen_count * day_rows)
    tail_count = acct_pnl.shape[1] // 40
    margin = jnp.mean(lax.top_k(-acct_pnl, tail_count)[0], axis=1)
    return (acct_pnl, margin)


def solution(mesh):
    placed = (
        P(("group", "scen"), None),
        P("group", None),
        P(),
        P(),
        P("scen"),
        P(("group", "inst", "acct")),
        P(None, ("group", "inst", "acct")),
        P(None, ("group", "inst", "acct")),
        P("group", ("inst", "acct")),
        P("group", ("inst", "acct")),
    )
    return jax.shard_map(
        body,
        mesh=mesh,
        in_specs=placed,
        out_specs=(
            P(("group", "scen", "inst", "acct"), None),
            P(("group", "scen", "inst", "acct")),
        ),
        check_vma=False,
    )
```

profile of v0, /device:TPU:0, one launch (start us, length us, event | category | flops | bytes accessed | tf_op | source)
XLA Modules:
  0.0 128.7 jit_solution(17734604005210548083)
XLA Ops:
  7.2 0.0 reduce-scatter.2.cloned.1.call-start
  7.3 0.7 negate_log-plus-one_fusion
  8.0 1.8 %multiply_multiply_fusion.1 = f32[512,1024]{1,0:T(8,128)S(1)} fusion(f32[512,1024]{1,0:T(8,128)} %param.12, f32[1024]{0:T(1024)} %param.14), kind=kLoop, calls=%fused_computation.63 | loop fusion | flops 1048576 | bytes 4198400 | tf_op jit(solution)/shard_map/mul | solution.py:66
  9.8 0.1 multiply_exponential_fusion.1
  10.0 1.6 %bitcast_multiply_fusion = f32[8,64,1024]{2,1,0:T(8,128)S(1)} fusion(f32[8,64,1024]{2,1,0:T(8,128)S(1)} %bitcast.47, f32[64,1024]{1,0:T(8,128)S(1)} %get-tuple-element.164, f32[64,1024]{1,0:T(8,128)S(1)} %get-tuple-element.163), kind=kOutput, calls=%fused_computation.58 | convolution fusion | flops 403705856 | bytes 4718592 | tf_op jit(solution)/shard_map/ij,bjf->bif/dot_general | solution.py:67
  11.6 0.2 multiply_reduce_fusion
  11.8 0.0 copy-start.3
  11.8 0.0 copy-start.6
  11.8 0.4 multiply_add_fusion
  12.2 0.0 copy-start
  12.2 1.3 %copy-done = f32[8,64,1024]{2,1,0:T(8,128)} copy-done((f32[8,64,1024]{2,1,0:T(8,128)}, f32[8,64,1024]{2,1,0:T(8,128)S(1)}, u32[]{:S(2)}) %copy-start) | copy-done | bytes 2097176
  13.6 0.0 copy-done.3
  13.6 0.0 copy-done.6
  13.6 14.9 %all-gather = f32[4096]{0:T(1024)S(1)} all-gather(f32[1024]{0:T(1024)S(1)} %get-tuple-element.162), channel_id=2, replica_groups=mesh['group'=2,'scen'=4,'inst'=2,'acct'=2] {'scen'}, dimensions={0}, use_global_device_ids=true | all-gather | bytes 20480 | tf_op jit(solution)/shard_map/all_gather | solution.py:11
  28.6 13.2 %all-gather.1 = f32[4,1,1024]{2,1,0:T(1,128)S(1)} all-gather(f32[1,1,1024]{2,1,0:T(1,128)S(1)} %get-tuple-element.158), channel_id=1, replica_groups=mesh['group'=2,'scen'=4,'inst'=2,'acct'=2] {'scen'}, dimensions={0}, use_global_device_ids=true | all-gather | bytes 20480 | tf_op jit(solution)/shard_map/all_gather | solution.py:11
  41.8 0.2 while.16
  42.0 11.7 %psum.7 = f32[1024]{0:T(1024)S(1)} all-reduce(f32[1024]{0:T(1024)S(1)} %get-tuple-element.161), channel_id=1, replica_groups=mesh['group'=2,'scen'=4,'inst'=2,'acct'=2] {'scen'}, use_global_device_ids=true, to_apply=%region_0.1 | all-reduce | flops 1024 | bytes 8192 | tf_op jit(solution)/shard_map/psum | solution.py:90
  53.7 0.0 copy-start.4
  53.7 0.0 copy-start.5
  53.7 0.0 copy-start.1
  53.7 3.4 %sqrt_multiply_fusion = f32[512,1024]{1,0:T(8,128)S(1)} fusion(f32[512,1024]{1,0:T(8,128)} %param.12, f32[1024]{0:T(1024)S(1)} %multiply_add_fusion.1, f32[1024]{0:T(1024)S(1)} %negate_log-plus-one_fusion, f32[512]{0:T(512)S(1)} %iota_add_fusion, f32[1024]{0:T(1024)S(1)} %psum.7, f32[8,64,1024]{2,1,0:T(8,128)} %copy-done), kind=kLoop, calls=%fused_computation.59 | loop fusion | flops 2621440 | bytes 6305792 | tf_op jit(solution)/shard_map/mul | solution.py:91
  57.2 1.3 %collective-permute-start = (f32[9,1024]{1,0:T(8,128)S(1)}, f32[9,1024]{1,0:T(8,128)S(1)}, u32[]{:S(2)}, u32[]{:S(2)}) collective-permute-start(f32[9,1024]{1,0:T(8,128)S(1)} %slice.51), channel_id=1, source_target_pairs={{0,4},{4,8},{8,12},{1,5},{5,9},{9,13},{2,6},{6,10},{10,14},{3,7},{... | collective-permute-start | bytes 110600 | tf_op jit(solution)/shard_map/ppermute | solution.py:26
  58.5 0.0 copy-done.4
  58.5 0.0 copy-done.5
  58.5 0.0 copy-done.1
  58.5 0.0 copy-start.7
  58.6 0.0 copy-start.2
  58.6 8.1 %broadcast_select_fusion.1 = (bf16[8,128,4096]{2,1,0:T(8,128)(2,1)}, bf16[8,128,4096]{2,1,0:T(8,128)(2,1)}) fusion(pred[8,4096]{1,0:T(8,128)(4,1)S(1)} %iota_compare_fusion, bf16[128,4096]{1,0:T(8,128)(2,1)S(1)} %copy-done.1, bf16[128,4096]{1,0:T(8,128)(2,1)} %param.19), kind=kLoop, calls=%fused_computation.17 | loop fusion | flops 8388608 | bytes 18907136 | tf_op jit(solution)/shard_map/jit(_where)/select_n | solution.py:104
  66.7 0.0 copy-done.7
  66.7 0.1 copy.17
  66.9 1.0 broadcast_in_dim.181
  67.9 0.6 broadcast_in_dim.182
  68.5 0.0 collective-permute-done
  68.5 0.0 copy-done.2
  68.5 3.3 %fusion.53 = (bf16[512,1024]{1,0:T(8,128)(2,1)S(1)}, f32[512,1024]{1,0:T(8,128)S(1)}) fusion(f32[512,1024]{1,0:T(8,128)S(1)} %sqrt_multiply_fusion, pred[512]{0:T(512)(128)(4,1)S(1)} %get-tuple-element.173, f32[9,1024]{1,0:T(8,128)S(1)} %broadcast_select_fusion.2, pred[512]{0:T(512)(128)(4,1)S(1)} %get-tuple-element.174, ...), kind=kLoop, calls=%fused_computation.102 | loop fusion | flops 15204352 | bytes 5284864 | tf_op jit(solution)/shard_map/convert_element_type | solution.py:98
  71.8 0.3 fusion.10
  72.1 0.0 copy-start.8
  72.1 12.7 %fusion.7 = bf16[512,4096,1,1]{1,0,3,2:T(8,128)(2,1)S(1)} fusion(bf16[1024,4096]{1,0:T(8,128)(2,1)} %bitcast.49, bf16[1024,4096]{1,0:T(8,128)(2,1)} %bitcast.48, bf16[512,1024]{1,0:T(8,128)(2,1)S(1)} %fusion.10, bf16[512,1024]{1,0:T(8,128)(2,1)S(1)} %get-tuple-element.151), kind=kOutput, calls=%fused_computation.19 | convolution fusion | flops 8629780480 | bytes 23068672 | tf_op jit(solution)/shard_map/dot_general | solution.py:107
  84.8 0.0 copy-done.8
  84.8 1.5 %convolution_bitcast_fusion = f32[4,4,8,512]{3,2,0,1:T(8,128)S(1)} fusion(bf16[512,4096,1,1]{1,0,3,2:T(8,128)(2,1)S(1)} %fusion.7, pred[4,4,8,4096]{3,2,1,0:T(8,128)(4,1)S(1)} %broadcast_in_dim.182, bf16[4,4,8,4096]{3,2,1,0:T(8,128)(2,1)S(1)} %bitcast.60), kind=kOutput, calls=%fused_computation.64 | convolution fusion | flops 537395200 | bytes 6029312 | tf_op jit(solution)/shard_map/knai,si->nkas/dot_general | solution.py:119
  86.3 0.7 copy.18
  87.0 0.0 reduce-scatter.2.cloned.1.call-update
  87.1 18.8 %reduce-scatter.2.cloned.1.call-done = f32[32,512]{1,0:T(8,128)} async-done(((f32[128,512]{1,0:T(8,128)}), f32[32,512]{1,0:T(8,128)}) %reduce-scatter.2.cloned.1.call-update) | async-done | bytes 65552 | tf_op jit(solution)/shard_map/reduce_scatter | solution.py:120
  105.8 10.4 %all_to_all.15 = f32[4,8,512]{2,1,0:T(8,128)S(1)} all-to-all(f32[4,8,512]{2,1,0:T(8,128)} %bitcast.56), channel_id=1, replica_groups=mesh['group'=2,'scen'=4,'inst'=2,'acct'=2] {'scen'}, dimensions={0} | all-to-all | bytes 131072 | tf_op jit(solution)/shard_map/all_to_all | solution.py:126
  116.2 4.4 %sort_prefixfusion = f32[8,51]{1,0:T(8,128)S(1)} fusion(f32[8,2048]{1,0:T(8,128)S(1)} %neg.16), kind=kCustom, calls=%top_k.9.sort_prefix | custom fusion | flops 229376 | bytes 67168 | tf_op jit(solution)/shard_map/top_k | solution.py:135
  120.6 0.2 reduce_sum.9
  120.7 0.5 broadcast_multiply_fusion
  121.3 0.6 copy.44
  (25 shorter events, 0.2 us)
Async XLA Ops:
  7.2 98.7 %reduce-scatter.2.cloned.1.call-start = ((), (), s32[]{:S(2)}) async-start(), calls=%async_computation.2 | async-start | bytes 327680 | tf_op jit(solution)/shard_map/reduce_scatter | solution.py:120
  11.8 1.8 %copy-start.3 = (f32[1024]{0:T(1024)S(1)}, f32[1024]{0:T(1024)}, u32[]{:S(2)}) copy-start(f32[1024]{0:T(1024)} %param.14) | copy-start | bytes 12292
  11.8 1.8 %copy-start.6 = (f32[1024]{0:T(1024)S(1)}, f32[1024]{0:T(1024)}, u32[]{:S(2)}) copy-start(f32[1024]{0:T(1024)} %param.15) | copy-start | bytes 12292
  12.2 1.4 %copy-start = (f32[8,64,1024]{2,1,0:T(8,128)}, f32[8,64,1024]{2,1,0:T(8,128)S(1)}, u32[]{:S(2)}) copy-start(f32[8,64,1024]{2,1,0:T(8,128)S(1)} %multiply_add_fusion) | copy-start | bytes 6291460
  53.7 4.8 %copy-start.4 = (s32[4096]{0:T(1024)S(1)}, s32[4096]{0:T(1024)}, u32[]{:S(2)}) copy-start(s32[4096]{0:T(1024)} %param.17) | copy-start | bytes 49156
  53.7 4.8 %copy-start.5 = (s32[128,32]{0,1:T(8,128)S(1)}, s32[128,32]{0,1:T(8,128)}, u32[]{:S(2)}) copy-start(s32[128,32]{0,1:T(8,128)} %param.21) | copy-start | bytes 49156
  53.7 4.8 %copy-start.1 = (bf16[128,4096]{1,0:T(8,128)(2,1)S(1)}, bf16[128,4096]{1,0:T(8,128)(2,1)}, u32[]{:S(2)}) copy-start(bf16[128,4096]{1,0:T(8,128)(2,1)} %param.18) | copy-start | bytes 3145732
  57.2 11.3 %collective-permute-start = (f32[9,1024]{1,0:T(8,128)S(1)}, f32[9,1024]{1,0:T(8,128)S(1)}, u32[]{:S(2)}, u32[]{:S(2)}) collective-permute-start(f32[9,1024]{1,0:T(8,128)S(1)} %slice.51), channel_id=1, source_target_pairs={{0,4},{4,8},{8,12},{1,5},{5,9},{9,13},{2,6},{6,10},{10,14},{3,7},{... | collective-permute-start | bytes 110600 | tf_op jit(solution)/shard_map/ppermute | solution.py:26
  58.5 8.2 %copy-start.7 = (s32[512]{0:T(512)S(1)}, s32[512]{0:T(512)}, u32[]{:S(2)}) copy-start(s32[512]{0:T(512)} %param.16) | copy-start | bytes 6148
  58.6 10.0 %copy-start.2 = (f32[9,1024]{1,0:T(8,128)S(1)}, f32[9,1024]{1,0:T(8,128)}, u32[]{:S(2)}) copy-start(f32[9,1024]{1,0:T(8,128)} %param.13) | copy-start | bytes 110596
  72.1 12.7 %copy-start.8 = (bf16[128,4096]{1,0:T(8,128)(2,1)S(1)}, bf16[128,4096]{1,0:T(8,128)(2,1)}, u32[]{:S(2)}) copy-start(bf16[128,4096]{1,0:T(8,128)(2,1)} %param.20) | copy-start | bytes 3145732
Sparse Core Ops, SparseCore 0:
  87.2 18.5 reduce-scatter.1
where the time goes:
time: 129 us
  blocking collectives  50.2 us (39%)
  other arithmetic  23.6 us (18%)
  waiting for transfers between devices  18.8 us (15%)
  matrix products  15.7 us (12%)
  between operations  14.4 us (11%)
  local copies, waits for them, and re-layouts  4.6 us (4%)
  starting transfers between devices  1.33 us (1%)
    all_gather x2, blocking collectives, carried_in(): pieces = jax.tree.map(lambda part: lax.all_gather(part, axis), value)  28.1 us
    reduce_scatter x1, waiting for transfers between devices, body(): lax.psum_scatter(acct_term.reshape(lax.axis_size(('inst', 'acct')) * shar...  18.8 us
    dot_general x1, matrix products, body(): jnp.dot(features, sensitivity, preferred_element_type=jnp.float32)  12.7 us
    psum x1, blocking collectives, body(): latest = lax.psum(own_part, 'scen')  11.7 us
    all_to_all x1, blocking collectives, body(): lax.all_to_all(summed.reshape(scen_count, acct_local, day_rows), 'scen',...  10.4 us
    select_n x1, other arithmetic, body(): jnp.where(chosen[:, None, :], delta_sens[None], 0)  8.14 us
    top_k x1, other arithmetic, body(): margin = jnp.mean(lax.top_k(-acct_pnl, tail_count)[0], axis=1)  4.37 us
    mul x1, other arithmetic, body(): scaled = returns * jnp.sqrt(latest / variance)  3.42 us
  transfers between devices with their start and end apart: 2, of which 1 were waited for; matrix products, arithmetic and copies ran while one was open for 8% of the time, Pallas kernels for 0%

commit v1 on v0

v1 whole, which is shorter than its diff:
```python
import functools

import jax
import jax.numpy as jnp
from jax import lax
from jax.experimental import pallas as pl
from jax.experimental.pallas import tpu as pltpu
from jax.sharding import PartitionSpec as P

WIN = 10
LANES = 128
SUB = 8
MESH = pl.DeviceIdType.MESH
NT = (((1,), (1,)), ((), ()))


def ipow(x, n):
    result = None
    while n:
        if n & 1:
            result = x if result is None else result * x
        n >>= 1
        if n:
            x = x * x
    return result


def kernel(
    sizes,
    ret_h, prior_h, dec_h, seed_h, off_h, bidx_h, delta_h, gamma_h, pos_h, pat_h,
    out_ref, marg_ref,
    ret, prior, dec, seed, off, bidx, sens, pos, pat,
    offb, state, start, ends, tail_out, tail_in, moves, wacc, whl, fcat,
    part, rs_in, summ, fin,
    in_sem, ret_sem, end_ss, end_rs, tail_ss, tail_rs, rs_ss, rs_rs, fin_ss, fin_rs,
):
    S, I, A, T = sizes
    owners = I * A
    rank = lax.axis_index("scen")
    inst, acct = lax.axis_index("inst"), lax.axis_index("acct")
    me = inst * A + acct
    C, R, _ = ret.shape
    L = R // SUB
    H = WIN - 1
    BW = delta_h.shape[0]
    accts, instr = pos.shape
    AL = accts // (S * owners)
    f32, bf16 = jnp.float32, jnp.bfloat16

    small = [
        pltpu.make_async_copy(src, dst, in_sem.at[n])
        for n, (src, dst) in enumerate(
            [(off_h, off), (dec_h, dec), (seed_h, seed), (prior_h, prior)]
        )
    ]
    late = [
        pltpu.make_async_copy(src, dst, in_sem.at[4 + n])
        for n, (src, dst) in enumerate(
            [
                (bidx_h, bidx),
                (pat_h, pat),
                (delta_h, sens.at[pl.ds(0, BW)]),
                (gamma_h, sens.at[pl.ds(BW, BW)]),
                (pos_h, pos),
            ]
        )
    ]
    cols = [
        pltpu.make_async_copy(
            ret_h.at[:, pl.ds(c * LANES, LANES)], ret.at[c], ret_sem.at[c]
        )
        for c in range(C)
    ]
    for copy in small + cols + late:
        copy.start()

    def owner_id(d):
        who = lax.rem(me + d, owners)
        return {"inst": who // A, "acct": lax.rem(who, A)}

    barrier = pltpu.get_barrier_semaphore()
    for d in range(1, S):
        pl.semaphore_signal(
            barrier, inc=1, device_id={"scen": lax.rem(rank + d, S)}, device_id_type=MESH
        )
    for d in range(1, owners):
        pl.semaphore_signal(barrier, inc=1, device_id=owner_id(d), device_id_type=MESH)

    for copy in small:
        copy.wait()
    row = lax.broadcasted_iota(jnp.int32, (R, R), 0)
    day = lax.broadcasted_iota(jnp.int32, (R, R), 1)
    pick = jnp.where((row % SUB) * L + row // SUB == day, 1.0, 0.0).astype(bf16)
    spread = jnp.broadcast_to(off[...].astype(f32), (LANES, R)).astype(bf16)
    offb[...] = lax.dot_general(pick, spread, NT, preferred_element_type=f32).reshape(
        L, SUB, LANES
    )

    keep_rows = 1.0 - dec[...]
    dec_c = [jnp.broadcast_to(dec[c : c + 1, :], (SUB, LANES)) for c in range(C)]
    keep_c = [1.0 - dec_c[c] for c in range(C)]
    for copy in cols:
        copy.wait()

    def scan(t, carry):
        new = []
        for c in range(C):
            x = ret[c, pl.ds(t, SUB, stride=L), :]
            v = keep_c[c] * carry[c] + dec_c[c] * x * x
            state[t, c] = v
            new.append(v)
        return tuple(new)

    zero = jnp.zeros((SUB, LANES), f32)
    last = lax.fori_loop(0, L, scan, (zero,) * C, unroll=4)

    sub = lax.broadcasted_iota(jnp.int32, (SUB, LANES), 0)
    for c in range(C):
        run = ipow(keep_c[c], L)
        x = last[c]
        for hop in (1, 2, 4):
            x = x + jnp.where(sub >= hop, run * pltpu.roll(x, hop, 0), 0.0)
            run = run * run
        ends[rank, c : c + 1, :] = x[SUB - 1 :, :]
        before = jnp.where(sub >= 1, pltpu.roll(x, 1, 0), 0.0)
        start[c] = before
        z = ipow(keep_c[c], L - H) * before
        for n in range(H):
            z = z * keep_c[c]
            v = state[L - H + n, c] + z
            tail_out[n, c : c + 1, :] = ret[c, R - H + n : R - H + n + 1, :]
            tail_out[H + n, c : c + 1, :] = v[SUB - 1 :, :]

    pl.semaphore_wait(barrier, S - 1 + owners - 1)
    sends = []
    for d in range(1, S):
        sends.append(
            pltpu.make_async_remote_copy(
                src_ref=ends.at[rank],
                dst_ref=ends.at[rank],
                send_sem=end_ss.at[d],
                recv_sem=end_rs.at[d],
                device_id={"scen": lax.rem(rank + d, S)},
                device_id_type=MESH,
            )
        )
    sends.append(
        pltpu.make_async_remote_copy(
            src_ref=tail_out,
            dst_ref=tail_in,
            send_sem=tail_ss,
            recv_sem=tail_rs,
            device_id={"scen": lax.rem(rank + 1, S)},
            device_id_type=MESH,
        )
    )
    for copy in sends:
        copy.start()

    for copy in late:
        copy.wait()
    AT = min(accts, 128)
    CH = min(instr, 512)
    blocks = pat.shape[1]
    PB = instr // blocks

    wacc[...] = jnp.zeros_like(wacc)

    def weigh(step, _):
        q, at = step // (accts // AT), lax.rem(step, accts // AT)
        rows = pl.ds(pl.multiple_of(at * AT, AT), AT)
        at_cols = pl.ds(pl.multiple_of(q * CH, CH), CH)
        ahead = lax.broadcasted_iota(jnp.int32, (blocks, CH), 1) + q * CH
        which = lax.broadcasted_iota(jnp.int32, (blocks, CH), 0) * PB
        widen = jnp.where((ahead >= which) & (ahead < which + PB), 1.0, 0.0).astype(bf16)
        holds = jnp.where(pat[rows, :] > 0, 1.0, 0.0).astype(bf16)
        mask = jnp.dot(holds, widen, preferred_element_type=f32).astype(bf16)
        held = pos[rows, at_cols] * mask
        own = bidx[:, at_cols]
        parts = [
            held * jnp.broadcast_to(jnp.where(own == b, 1.0, 0.0), (AT, CH)).astype(bf16)
            for b in range(C)
        ]
        got = lax.dot_general(
            jnp.concatenate(parts, axis=0), sens[:, at_cols], NT, preferred_element_type=f32
        )
        wacc[:, rows, :] += got.reshape(C, AT, 2 * BW)
        return 0

    lax.fori_loop(0, (instr // CH) * (accts // AT), weigh, 0)

    def split(step, _):
        c, at = step // (accts // AT), lax.rem(step, accts // AT)
        w = wacc[c, pl.ds(pl.multiple_of(at * AT, AT), AT), :]
        high = w.astype(bf16)
        whl[at, c, :AT, :] = high
        whl[at, c, AT:, :] = (w - high.astype(f32)).astype(bf16)
        return 0

    lax.fori_loop(0, C * (accts // AT), split, 0)

    for copy in sends:
        copy.wait()

    span = ipow(keep_rows, R)
    var = seed[...]
    entering = var
    entering_prev = var
    for n in range(S):
        entering = jnp.where(rank == n, var, entering)
        entering_prev = jnp.where(rank == n + 1, var, entering_prev)
        var = span * var + ends[n]
    root = jnp.sqrt(var)

    power = ipow(keep_rows, R - H)
    lead = []
    for n in range(H):
        power = power * keep_rows
        lead.append(
            tail_in[n] * (root * lax.rsqrt(tail_in[H + n] + power * entering_prev))
        )

    root_c, z0, heads = [], [], [[] for _ in range(C)]
    for c in range(C):
        root_b = jnp.broadcast_to(root[c : c + 1, :], (SUB, LANES))
        enter_b = jnp.broadcast_to(entering[c : c + 1, :], (SUB, LANES))
        run = ipow(keep_c[c], L)
        run_pow = jnp.ones((SUB, LANES), f32)
        for j in range(1, SUB):
            run_pow = jnp.where(sub >= j, run_pow * run, run_pow)
        z = start[c] + run_pow * enter_b
        root_c.append(root_b)
        z0.append(z)
        z = z * ipow(keep_c[c], L - H)
        for n in range(H):
            z = z * keep_c[c]
            t = L - H + n
            x = ret[c, pl.ds(t, SUB, stride=L), :]
            e = x * (root_b * lax.rsqrt(state[t, c] + z))
            first = jnp.where(
                rank == 0,
                prior[n : n + 1, c * LANES : (c + 1) * LANES],
                lead[n][c : c + 1, :],
            )
            heads[c].append(
                jnp.where(sub == 0, jnp.broadcast_to(first, (SUB, LANES)), pltpu.roll(e, 1, 0))
            )

    G, PAIR = 8, 2

    def window(group, block, carry):
        t0 = block * G
        new = []
        offs = [offb[t0 + i] for i in range(G)]
        for c, (z, e) in zip(group, carry):
            e = list(e)
            for i in range(G):
                z = z * keep_c[c]
                x = ret[c, pl.ds(t0 + i, SUB, stride=L), :]
                e.append(x * (root_c[c] * lax.rsqrt(state[t0 + i, c] + z)))
            new.append((z, tuple(e[G:])))
            two = {i: e[i] + e[i - 1] for i in range(3, G + H)}
            four = {i: two[i] + two[i - 2] for i in range(5, G + H)}
            for i in range(G):
                p = i + H
                total = four[p] + four[p - 4]
                total = total + jnp.where(offs[i] < 1.5, e[p - 8], 0.0)
                total = total + jnp.where(offs[i] < 0.5, e[p - 9], 0.0)
                moves[c, pl.ds(t0 + i, SUB, stride=L), :] = total
        return tuple(new)

    for g in range(0, C, PAIR):
        group = tuple(range(g, min(g + PAIR, C)))
        lax.fori_loop(
            0, L // G, functools.partial(window, group), tuple((z0[c], tuple(heads[c])) for c in group)
        )

    for c in range(C):
        m = moves[c]
        fcat[c, :, :LANES] = m.astype(bf16)
        fcat[c, :, LANES:] = (0.5 * m * m).astype(bf16)

    per = AT // AL

    def combine(at, _):
        both = jnp.zeros((2 * AT, R), f32)
        for c in range(C):
            both = both + lax.dot_general(
                whl[at, c], fcat[c], NT, preferred_element_type=f32
            )
        total = both[:AT] + both[AT:]
        for i in range(per):
            part[i % owners, at * (per // owners) + i // owners] = total[i * AL : (i + 1) * AL]
        return 0

    lax.fori_loop(0, accts // AT, combine, 0)

    hops = []
    for d in range(1, owners):
        hops.append(
            pltpu.make_async_remote_copy(
                src_ref=part.at[lax.rem(me + d, owners)],
                dst_ref=rs_in.at[d - 1],
                send_sem=rs_ss.at[d],
                recv_sem=rs_rs.at[d],
                device_id=owner_id(d),
                device_id_type=MESH,
            )
        )
    for copy in hops:
        copy.start()
    for copy in hops:
        copy.wait()
    for k in range(S):
        total = part[me, k]
        for d in range(1, owners):
            total = total + rs_in[d - 1, k]
        summ[k] = total

    outs = []
    for d in range(1, S):
        to = lax.rem(rank + d, S)
        outs.append(
            pltpu.make_async_remote_copy(
                src_ref=summ.at[to],
                dst_ref=fin.at[rank],
                send_sem=fin_ss.at[d],
                recv_sem=fin_rs.at[d],
                device_id={"scen": to},
                device_id_type=MESH,
            )
        )
    for copy in outs:
        copy.start()
    fin[rank] = summ[rank]
    for copy in outs:
        copy.wait()

    xs = []
    for k in range(S):
        y = fin[k]
        out_ref[:, k * R : (k + 1) * R] = y
        xs.extend(-y[:, i * LANES : (i + 1) * LANES] for i in range(R // LANES))

    groups = -(-T // LANES)
    each = len(xs) // groups
    peaks = []
    for g in range(groups):
        mine = xs[g * each : (g + 1) * each] if g < groups - 1 else xs[g * each :]
        peaks.append(functools.reduce(jnp.maximum, mine))
    high = jnp.max(functools.reduce(jnp.maximum, peaks), axis=1, keepdims=True)
    low = jnp.min(functools.reduce(jnp.minimum, peaks), axis=1, keepdims=True)
    low = jnp.broadcast_to(low, (AL, LANES))
    width = jnp.broadcast_to(high, (AL, LANES)) - low
    ways = 16
    for _ in range(6):
        width = width * (1.0 / ways)
        steps = jnp.zeros((AL, LANES), f32)
        for i in range(1, ways):
            bound = low + width * float(i)
            count = functools.reduce(
                jnp.add, [jnp.where(x >= bound, 1.0, 0.0) for x in xs]
            )
            count = jnp.sum(count, axis=1, keepdims=True)
            steps = steps + jnp.where(count >= float(T), 1.0, 0.0)
        low = low + width * steps
    above = functools.reduce(jnp.add, [jnp.maximum(x - low, 0.0) for x in xs])
    above = jnp.sum(above, axis=1, keepdims=True)
    marg_ref[...] = low + above * (1.0 / T)


def body(
    returns,
    prior,
    decay,
    seed_var,
    date_offsets,
    block_index,
    delta_sens,
    gamma_sens,
    positions,
    pattern,
):
    R, F = returns.shape
    S, I, A = lax.axis_size("scen"), lax.axis_size("inst"), lax.axis_size("acct")
    owners = I * A
    C, L, H = F // LANES, R // SUB, WIN - 1
    BW, instr = delta_sens.shape
    accts = positions.shape[0]
    AL = accts // (S * owners)
    AT = min(accts, 128)
    T = S * R // 40
    f32, bf16, i32 = jnp.float32, jnp.bfloat16, jnp.int32
    dma = pltpu.SemaphoreType.DMA
    acct_pnl, margin = pl.pallas_call(
        functools.partial(kernel, (S, I, A, T)),
        out_shape=(
            jax.ShapeDtypeStruct((AL, S * R), f32),
            jax.ShapeDtypeStruct((AL, LANES), f32),
        ),
        in_specs=[pl.BlockSpec(memory_space=pl.ANY)] * 10,
        out_specs=[pl.BlockSpec(memory_space=pltpu.VMEM)] * 2,
        scratch_shapes=[
            pltpu.VMEM((C, R, LANES), f32),
            pltpu.VMEM((H, F), f32),
            pltpu.VMEM((C, LANES), f32),
            pltpu.VMEM((C, LANES), f32),
            pltpu.VMEM((1, R), i32),
            pltpu.VMEM((1, instr), i32),
            pltpu.VMEM((2 * BW, instr), bf16),
            pltpu.VMEM((accts, instr), bf16),
            pltpu.VMEM(pattern.shape, i32),
            pltpu.VMEM((L, SUB, LANES), f32),
            pltpu.VMEM((L, C, SUB, LANES), f32),
            pltpu.VMEM((C, SUB, LANES), f32),
            pltpu.VMEM((S, C, LANES), f32),
            pltpu.VMEM((2 * H, C, LANES), f32),
            pltpu.VMEM((2 * H, C, LANES), f32),
            pltpu.VMEM((C, R, LANES), f32),
            pltpu.VMEM((C, accts, 2 * BW), f32),
            pltpu.VMEM((accts // AT, C, 2 * AT, 2 * BW), bf16),
            pltpu.VMEM((C, R, 2 * LANES), bf16),
            pltpu.VMEM((owners, S, AL, R), f32),
            pltpu.VMEM((owners - 1, S, AL, R), f32),
            pltpu.VMEM((S, AL, R), f32),
            pltpu.VMEM((S, AL, R), f32),
            dma((9,)),
            dma((C,)),
            dma((S,)),
            dma((S,)),
            dma,
            dma,
            dma((owners,)),
            dma((owners,)),
            dma((S,)),
            dma((S,)),
        ],
        compiler_params=pltpu.CompilerParams(
            collective_id=0, has_side_effects=True, vmem_limit_bytes=60 * 1024 * 1024
        ),
    )(
        returns,
        prior,
        decay.reshape(C, LANES),
        seed_var.reshape(C, LANES),
        date_offsets.reshape(1, R),
        block_index.reshape(1, instr),
        delta_sens,
        gamma_sens,
        positions,
        pattern,
    )
    return acct_pnl, margin[:, 0]


def solution(mesh):
    placed = (
        P(("group", "scen"), None),
        P("group", None),
        P(),
        P(),
        P("scen"),
        P(("group", "inst", "acct")),
        P(None, ("group", "inst", "acct")),
        P(None, ("group", "inst", "acct")),
        P("group", ("inst", "acct")),
        P("group", ("inst", "acct")),
    )
    return jax.shard_map(
        body,
        mesh=mesh,
        in_specs=placed,
        out_specs=(
            P(("group", "scen", "inst", "acct"), None),
            P(("group", "scen", "inst", "acct")),
        ),
        check_vma=False,
    )
```

time: 129 us -> 31.4 us (0.24)
  blocking collectives: 50.2 us -> 0 us
  Pallas kernels: 0 us -> 26.2 us
  other arithmetic: 23.6 us -> 0 us
  waiting for transfers between devices: 18.8 us -> 0 us
  matrix products: 15.7 us -> 0 us
  between operations: 14.4 us -> 0.64 us
  starting transfers between devices: 1.33 us -> 0 us
    all_gather x2 -> x0, blocking collectives: 28.1 us -> none  [carried_in(): pieces = jax.tree.map(lambda part: lax.all_gather(part, axis), value)]
    pallas_call x0 -> x1, Pallas kernels: none -> 26.2 us  [body(): pl.pallas_call(functools.partial(kernel, (S, I, A, T)), out_shape=(jax.Sh...]
    reduce_scatter x1 -> x0, waiting for transfers between devices: 18.8 us -> none  [body(): lax.psum_scatter(acct_term.reshape(lax.axis_size(('inst', 'acct')) * shar...]
    dot_general x3 -> x0, matrix products: 15.7 us -> none  [the longest x1 12.7 us: body(): jnp.dot(features, sensitivity, preferred_element_type=jnp.float32)]
    psum x1 -> x0, blocking collectives: 11.7 us -> none  [body(): latest = lax.psum(own_part, 'scen')]
    all_to_all x1 -> x0, blocking collectives: 10.4 us -> none  [body(): lax.all_to_all(summed.reshape(scen_count, acct_local, day_rows), 'scen',...]
    select_n x5 -> x0, other arithmetic: 8.18 us -> none  [the longest x1 8.14 us: body(): jnp.where(chosen[:, None, :], delta_sens[None], 0)]
    mul x3 -> x0, other arithmetic: 5.26 us -> none  [the longest x1 3.42 us: body(): scaled = returns * jnp.sqrt(latest / variance)]
  transfers between devices with their start and end apart: 2 -> 0, of which waited for: 1 -> 0; matrix products, arithmetic and copies ran while one was open for 8% -> 0% of each run, Pallas kernels for 0% -> 0%
where the time goes in v1:
time: 31.4 us; the launch traced here: 31.1 us
  Pallas kernels  26.2 us (83%)
  local copies, waits for them, and re-layouts  4.22 us (13%)
  between operations  0.64 us (2%)
    pallas_call x1, Pallas kernels, body(): pl.pallas_call(functools.partial(kernel, (S, I, A, T)), out_shape=(jax.Sh...  26.2 us
    unnamed x2, local copies, waits for them, and re-layouts  2.92 us
    slice x1, local copies, waits for them, and re-layouts, body(): return (acct_pnl, margin[:, 0])  1.3 us

profile of v1, /device:TPU:0, one launch (start us, length us, event | category | flops | bytes accessed | tf_op | source)
XLA Modules:
  0.0 31.1 jit_solution(7825686154879632692)
XLA Ops:
  0.6 1.4 %copy.13.pat_h = s32[128,32]{1,0:T(8,128)} copy(s32[128,32]{0,1:T(8,128)} %param.19) | data formatting | bytes 32768 | tf_op args[9]
  2.1 26.2 %shard_map.113 = (f32[8,2048]{1,0:T(8,128)}, f32[8,128]{1,0:T(8,128)}) custom-call(f32[512,1024]{1,0:T(8,128)} %ret_h.1, f32[9,1024]{1,0:T(8,128)} %prior_h.1, f32[8,128]{1,0:T(8,128)} %bitcast.5, f32[8,128]{1,0:T(8,128)} %bitcast.6, s32[1,512]{1,0:T(1,128)} %bitcast.7, s32[1,4096]{1,0:T(1,128)} %bitcast.4, bf16[128,4096]{1,0:T(8,128)(2,1)} %delta_h.1, ...), custom_call_target="tpu_custom_call" | custom-call | tf_op jit(solution)/shard_map/pallas_call | solution.py:395
  28.3 1.3 %slice_reduce_fusion = f32[8]{0:T(128)} fusion(f32[8,128]{1,0:T(8,128)} %get-tuple-element.5), kind=kLoop, calls=%fused_computation | loop fusion | bytes 64 | tf_op jit(solution)/shard_map/slice | solution.py:453
  29.6 1.5 %copy.15 = f32[8,2048]{1,0:T(8,128)} copy(f32[8,2048]{1,0:T(8,128)} %get-tuple-element.8) | data formatting | bytes 131072

commit v2 on v1

--- a/solution.py
+++ b/solution.py
@@ -28,8 +28,8 @@
 def kernel(
     sizes,
     ret_h, prior_h, dec_h, seed_h, off_h, bidx_h, delta_h, gamma_h, pos_h, pat_h,
-    out_ref, marg_ref,
-    ret, prior, dec, seed, off, bidx, sens, pos, pat,
+    out_ref,
+    pick, ret, prior, dec, seed, off, bidx, sens, pos, pat,
     offb, state, start, ends, tail_out, tail_in, moves, wacc, whl, fcat,
     part, rs_in, summ, fin,
     in_sem, ret_sem, end_ss, end_rs, tail_ss, tail_rs, rs_ss, rs_rs, fin_ss, fin_rs,
@@ -39,8 +39,8 @@
     rank = lax.axis_index("scen")
     inst, acct = lax.axis_index("inst"), lax.axis_index("acct")
     me = inst * A + acct
-    C, R, _ = ret.shape
-    L = R // SUB
+    L, _, F = ret.shape
+    C, R = F // LANES, L * SUB
     H = WIN - 1
     BW = delta_h.shape[0]
     accts, instr = pos.shape
@@ -67,9 +67,9 @@
     ]
     cols = [
         pltpu.make_async_copy(
-            ret_h.at[:, pl.ds(c * LANES, LANES)], ret.at[c], ret_sem.at[c]
-        )
-        for c in range(C)
+            ret_h.at[pl.ds(j * L, L), :], ret.at[:, j, :], ret_sem.at[j]
+        )
+        for j in range(SUB)
     ]
     for copy in small + cols + late:
         copy.start()
@@ -90,9 +90,9 @@
         copy.wait()
     row = lax.broadcasted_iota(jnp.int32, (R, R), 0)
     day = lax.broadcasted_iota(jnp.int32, (R, R), 1)
-    pick = jnp.where((row % SUB) * L + row // SUB == day, 1.0, 0.0).astype(bf16)
+    pick[...] = jnp.where((row % SUB) * L + row // SUB == day, 1.0, 0.0).astype(bf16)
     spread = jnp.broadcast_to(off[...].astype(f32), (LANES, R)).astype(bf16)
-    offb[...] = lax.dot_general(pick, spread, NT, preferred_element_type=f32).reshape(
+    offb[...] = lax.dot_general(pick[...], spread, NT, preferred_element_type=f32).reshape(
         L, SUB, LANES
     )
 
@@ -105,7 +105,7 @@
     def scan(t, carry):
         new = []
         for c in range(C):
-            x = ret[c, pl.ds(t, SUB, stride=L), :]
+            x = ret[t, :, c * LANES : (c + 1) * LANES]
             v = keep_c[c] * carry[c] + dec_c[c] * x * x
             state[t, c] = v
             new.append(v)
@@ -128,7 +128,7 @@
         for n in range(H):
             z = z * keep_c[c]
             v = state[L - H + n, c] + z
-            tail_out[n, c : c + 1, :] = ret[c, R - H + n : R - H + n + 1, :]
+            tail_out[n, c : c + 1, :] = ret[L - H + n, SUB - 1 :, c * LANES : (c + 1) * LANES]
             tail_out[H + n, c : c + 1, :] = v[SUB - 1 :, :]
 
     pl.semaphore_wait(barrier, S - 1 + owners - 1)
@@ -160,8 +160,8 @@
     for copy in late:
         copy.wait()
     AT = min(accts, 128)
-    CH = min(instr, 512)
-    blocks = pat.shape[1]
+    CH = min(instr, 1024)
+    blocks = pat.shape[0]
     PB = instr // blocks
 
     wacc[...] = jnp.zeros_like(wacc)
@@ -173,8 +173,10 @@
         ahead = lax.broadcasted_iota(jnp.int32, (blocks, CH), 1) + q * CH
         which = lax.broadcasted_iota(jnp.int32, (blocks, CH), 0) * PB
         widen = jnp.where((ahead >= which) & (ahead < which + PB), 1.0, 0.0).astype(bf16)
-        holds = jnp.where(pat[rows, :] > 0, 1.0, 0.0).astype(bf16)
-        mask = jnp.dot(holds, widen, preferred_element_type=f32).astype(bf16)
+        holds = jnp.where(pat[:, rows] > 0, 1.0, 0.0).astype(bf16)
+        mask = lax.dot_general(
+            holds, widen, (((0,), (0,)), ((), ())), preferred_element_type=f32
+        ).astype(bf16)
         held = pos[rows, at_cols] * mask
         own = bidx[:, at_cols]
         parts = [
@@ -235,7 +237,7 @@
         for n in range(H):
             z = z * keep_c[c]
             t = L - H + n
-            x = ret[c, pl.ds(t, SUB, stride=L), :]
+            x = ret[t, :, c * LANES : (c + 1) * LANES]
             e = x * (root_b * lax.rsqrt(state[t, c] + z))
             first = jnp.where(
                 rank == 0,
@@ -256,7 +258,7 @@
             e = list(e)
             for i in range(G):
                 z = z * keep_c[c]
-                x = ret[c, pl.ds(t0 + i, SUB, stride=L), :]
+                x = ret[t0 + i, :, c * LANES : (c + 1) * LANES]
                 e.append(x * (root_c[c] * lax.rsqrt(state[t0 + i, c] + z)))
             new.append((z, tuple(e[G:])))
             two = {i: e[i] + e[i - 1] for i in range(3, G + H)}
@@ -266,7 +268,7 @@
                 total = four[p] + four[p - 4]
                 total = total + jnp.where(offs[i] < 1.5, e[p - 8], 0.0)
                 total = total + jnp.where(offs[i] < 0.5, e[p - 9], 0.0)
-                moves[c, pl.ds(t0 + i, SUB, stride=L), :] = total
+                moves[c, t0 + i] = total
         return tuple(new)
 
     for g in range(0, C, PAIR):
@@ -276,7 +278,7 @@
         )
 
     for c in range(C):
-        m = moves[c]
+        m = moves[c].reshape(R, LANES)
         fcat[c, :, :LANES] = m.astype(bf16)
         fcat[c, :, LANES:] = (0.5 * m * m).astype(bf16)
 
@@ -311,11 +313,19 @@
         copy.start()
     for copy in hops:
         copy.wait()
-    for k in range(S):
-        total = part[me, k]
-        for d in range(1, owners):
-            total = total + rs_in[d - 1, k]
-        summ[k] = total
+    total = part[me]
+    for d in range(1, owners):
+        total = total + rs_in[d - 1]
+    rows = total.reshape(S * AL, R)
+    pieces = []
+    for _ in range(3):
+        piece = rows.astype(bf16)
+        pieces.append(piece)
+        rows = rows - piece.astype(f32)
+    first, second, third = [
+        jnp.dot(piece, pick[...], preferred_element_type=f32) for piece in pieces
+    ]
+    summ[...] = ((first + second) + third).reshape(S, AL, R)
 
     outs = []
     for d in range(1, S):
@@ -335,7 +345,12 @@
     fin[rank] = summ[rank]
     for copy in outs:
         copy.wait()
-
+    out_ref[...] = fin[...]
+
+
+def tail_kernel(T, fin, out_ref, marg_ref):
+    S, AL, R = fin.shape
+    f32 = jnp.float32
     xs = []
     for k in range(S):
         y = fin[k]
@@ -366,7 +381,10 @@
         low = low + width * steps
     above = functools.reduce(jnp.add, [jnp.maximum(x - low, 0.0) for x in xs])
     above = jnp.sum(above, axis=1, keepdims=True)
-    marg_ref[...] = low + above * (1.0 / T)
+    short = low + above * (1.0 / T)
+    lane = lax.broadcasted_iota(jnp.int32, (AL, LANES), 1)
+    mine = lane == lax.broadcasted_iota(jnp.int32, (AL, LANES), 0)
+    marg_ref[...] = jnp.sum(jnp.where(mine, short, 0.0), axis=0)[:AL]
 
 
 def body(
@@ -392,16 +410,14 @@
     T = S * R // 40
     f32, bf16, i32 = jnp.float32, jnp.bfloat16, jnp.int32
     dma = pltpu.SemaphoreType.DMA
-    acct_pnl, margin = pl.pallas_call(
+    joined = pl.pallas_call(
         functools.partial(kernel, (S, I, A, T)),
-        out_shape=(
-            jax.ShapeDtypeStruct((AL, S * R), f32),
-            jax.ShapeDtypeStruct((AL, LANES), f32),
-        ),
+        out_shape=jax.ShapeDtypeStruct((S, AL, R), f32),
         in_specs=[pl.BlockSpec(memory_space=pl.ANY)] * 10,
-        out_specs=[pl.BlockSpec(memory_space=pltpu.VMEM)] * 2,
+        out_specs=pl.BlockSpec(memory_space=pltpu.VMEM),
         scratch_shapes=[
-            pltpu.VMEM((C, R, LANES), f32),
+            pltpu.VMEM((R, R), bf16),
+            pltpu.VMEM((L, SUB, F), f32),
             pltpu.VMEM((H, F), f32),
             pltpu.VMEM((C, LANES), f32),
             pltpu.VMEM((C, LANES), f32),
@@ -409,14 +425,14 @@
             pltpu.VMEM((1, instr), i32),
             pltpu.VMEM((2 * BW, instr), bf16),
             pltpu.VMEM((accts, instr), bf16),
-            pltpu.VMEM(pattern.shape, i32),
+            pltpu.VMEM(pattern.shape[::-1], i32),
             pltpu.VMEM((L, SUB, LANES), f32),
             pltpu.VMEM((L, C, SUB, LANES), f32),
             pltpu.VMEM((C, SUB, LANES), f32),
             pltpu.VMEM((S, C, LANES), f32),
             pltpu.VMEM((2 * H, C, LANES), f32),
             pltpu.VMEM((2 * H, C, LANES), f32),
-            pltpu.VMEM((C, R, LANES), f32),
+            pltpu.VMEM((C, L, SUB, LANES), f32),
             pltpu.VMEM((C, accts, 2 * BW), f32),
             pltpu.VMEM((accts // AT, C, 2 * AT, 2 * BW), bf16),
             pltpu.VMEM((C, R, 2 * LANES), bf16),
@@ -425,7 +441,7 @@
             pltpu.VMEM((S, AL, R), f32),
             pltpu.VMEM((S, AL, R), f32),
             dma((9,)),
-            dma((C,)),
+            dma((SUB,)),
             dma((S,)),
             dma((S,)),
             dma,
@@ -448,9 +464,17 @@
         delta_sens,
         gamma_sens,
         positions,
-        pattern,
+        pattern.T,
     )
-    return acct_pnl, margin[:, 0]
+    return pl.pallas_call(
+        functools.partial(tail_kernel, T),
+        out_shape=(
+            jax.ShapeDtypeStruct((AL, S * R), f32),
+            jax.ShapeDtypeStruct((AL,), f32),
+        ),
+        in_specs=[pl.BlockSpec(memory_space=pltpu.VMEM)],
+        out_specs=[pl.BlockSpec(memory_space=pltpu.VMEM)] * 2,
+    )(joined)
 
 
 def solution(mesh):

time: 31.4 us -> 24.7 us (0.79)
  local copies, waits for them, and re-layouts: 4.22 us -> 0 us
  Pallas kernels: 26.2 us -> 23.9 us
    unnamed x2 -> x0, local copies, waits for them, and re-layouts: 2.92 us -> none
    pallas_call x1 -> x2, Pallas kernels: 26.2 us -> 23.9 us  [the longest x1 21.3 us: body(): pl.pallas_call(functools.partial(kernel, (S, I, A, T)), out_shape=jax.Sha...]
    slice x1 -> x0, local copies, waits for them, and re-layouts: 1.3 us -> none  [body(): return (acct_pnl, margin[:, 0])]
where the time goes in v2:
time: 24.7 us; the launch traced here: 24.6 us
  Pallas kernels  23.9 us (97%)
  between operations  0.64 us (3%)
    pallas_call x1, Pallas kernels, body(): pl.pallas_call(functools.partial(kernel, (S, I, A, T)), out_shape=jax.Sha...  21.3 us
    pallas_call x1, Pallas kernels, body(): pl.pallas_call(functools.partial(tail_kernel, T), out_shape=(jax.ShapeDty...  2.64 us

profile of v2, /device:TPU:0, one launch (start us, length us, event | category | flops | bytes accessed | tf_op | source)
XLA Modules:
  0.0 24.6 jit_solution(11164056772198808158)
XLA Ops:
  0.6 21.3 %shard_map.113.fin = f32[4,8,512]{2,1,0:T(8,128)} custom-call(f32[512,1024]{1,0:T(8,128)} %ret_h.1, f32[9,1024]{1,0:T(8,128)} %prior_h.1, f32[8,128]{1,0:T(8,128)} %bitcast.7, f32[8,128]{1,0:T(8,128)} %bitcast.8, s32[1,512]{1,0:T(1,128)} %bitcast.9, s32[1,4096]{1,0:T(1,128)} %bitcast.5, bf16[128,4096]{1,0:T(8,128)(2,1)} %delta_h.1, ...), custom_call_target="tpu_custom_call" | custom-call | tf_op jit(solution)/shard_map/pallas_call | solution.py:413
  21.9 2.6 %shard_map.114 = (f32[8,2048]{1,0:T(8,128)}, f32[8]{0:T(128)}) custom-call(f32[4,8,512]{2,1,0:T(8,128)} %shard_map.113.fin), custom_call_target="tpu_custom_call" | custom-call | tf_op jit(solution)/shard_map/pallas_call | solution.py:469

commit v3 on v2

--- a/solution.py
+++ b/solution.py
@@ -8,6 +8,7 @@
 from jax.sharding import PartitionSpec as P
 
 WIN = 10
+HALVES = 2
 LANES = 128
 SUB = 8
 MESH = pl.DeviceIdType.MESH
@@ -271,81 +272,95 @@
                 moves[c, t0 + i] = total
         return tuple(new)
 
-    for g in range(0, C, PAIR):
-        group = tuple(range(g, min(g + PAIR, C)))
-        lax.fori_loop(
-            0, L // G, functools.partial(window, group), tuple((z0[c], tuple(heads[c])) for c in group)
-        )
-
-    for c in range(C):
-        m = moves[c].reshape(R, LANES)
-        fcat[c, :, :LANES] = m.astype(bf16)
-        fcat[c, :, LANES:] = (0.5 * m * m).astype(bf16)
-
     per = AT // AL
-
-    def combine(at, _):
-        both = jnp.zeros((2 * AT, R), f32)
+    RH = R // HALVES
+    ahead_of = [(z0[c], tuple(heads[c])) for c in range(C)]
+    hops = []
+    for half in range(HALVES):
+        first, past = half * (L // G) // HALVES, (half + 1) * (L // G) // HALVES
+        for g in range(0, C, PAIR):
+            group = tuple(range(g, min(g + PAIR, C)))
+            ahead_of[g : g + PAIR] = lax.fori_loop(
+                first, past, functools.partial(window, group), tuple(ahead_of[g : g + PAIR])
+            )
         for c in range(C):
-            both = both + lax.dot_general(
-                whl[at, c], fcat[c], NT, preferred_element_type=f32
-            )
-        total = both[:AT] + both[AT:]
-        for i in range(per):
-            part[i % owners, at * (per // owners) + i // owners] = total[i * AL : (i + 1) * AL]
-        return 0
-
-    lax.fori_loop(0, accts // AT, combine, 0)
-
-    hops = []
-    for d in range(1, owners):
+            m = moves[c, half * (L // HALVES) : (half + 1) * (L // HALVES)].reshape(RH, LANES)
+            fcat[half, c, :, :LANES] = m.astype(bf16)
+            fcat[half, c, :, LANES:] = (0.5 * m * m).astype(bf16)
+
+        def combine(at, _, half=half):
+            both = jnp.zeros((2 * AT, RH), f32)
+            for c in range(C):
+                both = both + lax.dot_general(
+                    whl[at, c], fcat[half, c], NT, preferred_element_type=f32
+                )
+            total = both[:AT] + both[AT:]
+            for i in range(per):
+                part[half, i % owners, at * (per // owners) + i // owners] = total[
+                    i * AL : (i + 1) * AL
+                ]
+            return 0
+
+        lax.fori_loop(0, accts // AT, combine, 0)
         hops.append(
-            pltpu.make_async_remote_copy(
-                src_ref=part.at[lax.rem(me + d, owners)],
-                dst_ref=rs_in.at[d - 1],
-                send_sem=rs_ss.at[d],
-                recv_sem=rs_rs.at[d],
-                device_id=owner_id(d),
-                device_id_type=MESH,
-            )
-        )
-    for copy in hops:
-        copy.start()
-    for copy in hops:
-        copy.wait()
-    total = part[me]
-    for d in range(1, owners):
-        total = total + rs_in[d - 1]
-    rows = total.reshape(S * AL, R)
-    pieces = []
-    for _ in range(3):
-        piece = rows.astype(bf16)
-        pieces.append(piece)
-        rows = rows - piece.astype(f32)
-    first, second, third = [
-        jnp.dot(piece, pick[...], preferred_element_type=f32) for piece in pieces
-    ]
-    summ[...] = ((first + second) + third).reshape(S, AL, R)
+            [
+                pltpu.make_async_remote_copy(
+                    src_ref=part.at[half, lax.rem(me + d, owners)],
+                    dst_ref=rs_in.at[half, d - 1],
+                    send_sem=rs_ss.at[half, d],
+                    recv_sem=rs_rs.at[half, d],
+                    device_id=owner_id(d),
+                    device_id_type=MESH,
+                )
+                for d in range(1, owners)
+            ]
+        )
+        for copy in hops[half]:
+            copy.start()
 
     outs = []
-    for d in range(1, S):
-        to = lax.rem(rank + d, S)
+    for half in range(HALVES):
+        for copy in hops[half]:
+            copy.wait_recv()
+        total = part[half, me]
+        for d in range(1, owners):
+            total = total + rs_in[half, d - 1]
+        summ[half] = total
         outs.append(
-            pltpu.make_async_remote_copy(
-                src_ref=summ.at[to],
-                dst_ref=fin.at[rank],
-                send_sem=fin_ss.at[d],
-                recv_sem=fin_rs.at[d],
-                device_id={"scen": to},
-                device_id_type=MESH,
-            )
-        )
-    for copy in outs:
-        copy.start()
-    fin[rank] = summ[rank]
-    for copy in outs:
-        copy.wait()
-    out_ref[...] = fin[...]
+            [
+                pltpu.make_async_remote_copy(
+                    src_ref=summ.at[half, lax.rem(rank + d, S)],
+                    dst_ref=fin.at[half, rank],
+                    send_sem=fin_ss.at[half, d],
+                    recv_sem=fin_rs.at[half, d],
+                    device_id={"scen": lax.rem(rank + d, S)},
+                    device_id_type=MESH,
+                )
+                for d in range(1, S)
+            ]
+        )
+        for copy in outs[half]:
+            copy.start()
+        fin[half, rank] = summ[half, rank]
+    dated = jnp.zeros((S * AL, R), f32)
+    for half in range(HALVES):
+        for copy in outs[half]:
+            copy.wait()
+        rows = fin[half].reshape(S * AL, RH)
+        pieces = []
+        for _ in range(3):
+            piece = rows.astype(bf16)
+            pieces.append(piece)
+            rows = rows - piece.astype(f32)
+        days = pick[half * RH : (half + 1) * RH, :]
+        one, two, three = [
+            jnp.dot(piece, days, preferred_element_type=f32) for piece in pieces
+        ]
+        dated = dated + ((one + two) + three)
+    out_ref[...] = dated.reshape(S, AL, R)
+    for copies in hops:
+        for copy in copies:
+            copy.wait_send()
 
 
 def tail_kernel(T, fin, out_ref, marg_ref):
@@ -435,21 +450,21 @@
             pltpu.VMEM((C, L, SUB, LANES), f32),
             pltpu.VMEM((C, accts, 2 * BW), f32),
             pltpu.VMEM((accts // AT, C, 2 * AT, 2 * BW), bf16),
-            pltpu.VMEM((C, R, 2 * LANES), bf16),
-            pltpu.VMEM((owners, S, AL, R), f32),
-            pltpu.VMEM((owners - 1, S, AL, R), f32),
-            pltpu.VMEM((S, AL, R), f32),
-            pltpu.VMEM((S, AL, R), f32),
+            pltpu.VMEM((HALVES, C, R // HALVES, 2 * LANES), bf16),
+            pltpu.VMEM((HALVES, owners, S, AL, R // HALVES), f32),
+            pltpu.VMEM((HALVES, owners - 1, S, AL, R // HALVES), f32),
+            pltpu.VMEM((HALVES, S, AL, R // HALVES), f32),
+            pltpu.VMEM((HALVES, S, AL, R // HALVES), f32),
             dma((9,)),
             dma((SUB,)),
             dma((S,)),
             dma((S,)),
             dma,
             dma,
-            dma((owners,)),
-            dma((owners,)),
-            dma((S,)),
-            dma((S,)),
+            dma((HALVES, owners)),
+            dma((HALVES, owners)),
+            dma((HALVES, S)),
+            dma((HALVES, S)),
         ],
         compiler_params=pltpu.CompilerParams(
             collective_id=0, has_side_effects=True, vmem_limit_bytes=60 * 1024 * 1024

time: 24.7 us -> 24.4 us (0.988)
  Pallas kernels: 23.9 us -> 23.5 us
    pallas_call x1, Pallas kernels: 21.3 us -> 20.9 us  [body(): pl.pallas_call(functools.partial(kernel, (S, I, A, T)), out_shape=jax.Sha...]
where the time goes in v3:
time: 24.4 us; the launch traced here: 24.2 us
  Pallas kernels  23.5 us (96%)
  between operations  0.64 us (3%)
    pallas_call x1, Pallas kernels, body(): pl.pallas_call(functools.partial(kernel, (S, I, A, T)), out_shape=jax.Sha...  20.9 us
    pallas_call x1, Pallas kernels, body(): pl.pallas_call(functools.partial(tail_kernel, T), out_shape=(jax.ShapeDty...  2.64 us

profile of v3, /device:TPU:0, one launch (start us, length us, event | category | flops | bytes accessed | tf_op | source)
XLA Modules:
  0.0 24.2 jit_solution(11595778598728662388)
XLA Ops:
  0.6 20.9 %shard_map.113.fin = f32[4,8,512]{2,1,0:T(8,128)} custom-call(f32[512,1024]{1,0:T(8,128)} %ret_h.1, f32[9,1024]{1,0:T(8,128)} %prior_h.1, f32[8,128]{1,0:T(8,128)} %bitcast.7, f32[8,128]{1,0:T(8,128)} %bitcast.8, s32[1,512]{1,0:T(1,128)} %bitcast.9, s32[1,4096]{1,0:T(1,128)} %bitcast.5, bf16[128,4096]{1,0:T(8,128)(2,1)} %delta_h.1, ...), custom_call_target="tpu_custom_call" | custom-call | tf_op jit(solution)/shard_map/pallas_call | solution.py:428
  21.5 2.6 %shard_map.114 = (f32[8,2048]{1,0:T(8,128)}, f32[8]{0:T(128)}) custom-call(f32[4,8,512]{2,1,0:T(8,128)} %shard_map.113.fin), custom_call_target="tpu_custom_call" | custom-call | tf_op jit(solution)/shard_map/pallas_call | solution.py:484
